TPU v7x, 256 devices: a whole 4x4x8 slice. The times are simulated.
256 devices in a mesh: pipe: 4 (over y), fsdp: 32 (over x_hi, z, core), tensor: 2 (over x_lo).
Axes of the slice: x: 4 (x_hi: 2, x_lo: 2; x = x_hi * 2 + x_lo), y: 4, z: 8, core: 2. Of those that a mesh axis runs over, the one named last changes fastest.
Arguments:
- tokens: bfloat16 [6144, 4096], P('fsdp', 'tensor'), may hold values from -8 to 8
- norm_gains: float32 [4, 4096], P('pipe'), may hold values from 0.1 to 1.9
- q_blocks: bfloat16 [4, 4, 16, 256, 256], P('pipe', None, 'tensor', 'fsdp'), may hold values from -1 to 1
- k_blocks: bfloat16 [4, 4, 16, 256, 256], P('pipe', None, 'tensor', 'fsdp'), may hold values from -1 to 1
- v_blocks: bfloat16 [4, 4, 16, 256, 256], P('pipe', None, 'tensor', 'fsdp'), may hold values from -0.1875 to 0.1875
- o_blocks: bfloat16 [4, 4, 16, 256, 256], P('pipe', 'tensor', None, 'fsdp'), may hold values from -0.1875 to 0.1875
- q_rows: int32 [4, 4, 16], P('pipe', None, 'tensor'), may hold values from 0 to 15, as said below
- k_rows: int32 [4, 4, 16], P('pipe', None, 'tensor'), may hold values from 0 to 15, as said below
- v_rows: int32 [4, 4, 16], P('pipe', None, 'tensor'), may hold values from 0 to 15, as said below
- o_rows: int32 [4, 4, 16], P('pipe', 'tensor'), may hold values from 0 to 7, as said below
- mask_blocks: int32 [96, 4, 4], P('fsdp'), may hold values from 0 to 1, as said below
Outputs:
- activations: bfloat16 [4, 6144, 4096], P('pipe', 'fsdp', 'tensor')
Inputs may be any that keep to these rules, and one draw needn't show every extreme that they name: `q_rows`: for each section and column block the 4 listed input blocks are distinct. `k_rows`: for each section and column block the 4 listed input blocks are distinct. `v_rows`: for each section and column block the 4 listed input blocks are distinct. `o_rows`: entries k and k2 with k // 2 == k2 // 2 name distinct head blocks of one column block. Every diagonal block mask_blocks[n, i, i] is 1.
All inputs are finite; a program needn't handle non-finite values.
Results may differ from a plain program's by a relative error of at most 0.017.
Values may be sent and summed in bfloat16 or wider, within the bound.
A program may use at most 64 MiB of HBM per device.

v0:
```python
import jax
import jax.numpy as jnp
from jax import lax
from jax.sharding import PartitionSpec as P

HD = 128
MBLK = 16


def from_behind(value, axis, steps):
    count = lax.axis_size(axis)
    initial, last = (max(0, -steps), min(count, count - steps))
    return lax.ppermute(value, axis, [(source, source + steps) for source in range(initial, last)])


def block_project(in_rows, blocks, pattern):
    row_count = in_rows.shape[0]
    block_width = blocks.shape[-1]
    row_blocks = in_rows.reshape(row_count, -1, block_width)
    picked = row_blocks[:, pattern]
    product = jnp.einsum("rpcb,pcbe->rce", picked, blocks, preferred_element_type=jnp.float32)
    return product.reshape(row_count, -1)


def run_layer(
    u_half, mask_now, gain_row, q_full, k_full, v_full, out_weights, q_rows, k_rows, v_rows, o_rows
):
    gathered = lax.all_gather(u_half, "tensor", axis=1, tiled=True)
    values = gathered.astype(jnp.float32)
    inv_rms = lax.rsqrt(jnp.mean(values * values, axis=-1, keepdims=True) + 1e-05)
    normed = (values * inv_rms * gain_row[None, :]).astype(jnp.bfloat16)
    queries = block_project(normed, q_full, q_rows).astype(jnp.bfloat16)
    keys_proj = block_project(normed, k_full, k_rows).astype(jnp.bfloat16)
    values_proj = block_project(normed, v_full, v_rows).astype(jnp.bfloat16)
    o_full = out_weights()
    row_count = queries.shape[0]
    head_count = queries.shape[1] // HD
    head_shape = (row_count, head_count, HD)
    scores = jnp.einsum(
        "qhd,khd->hqk",
        queries.reshape(head_shape),
        keys_proj.reshape(head_shape),
        preferred_element_type=jnp.float32,
    ) * HD ** (-0.5)
    allowed = jnp.repeat(jnp.repeat(mask_now, MBLK, axis=0), MBLK, axis=1) == 1
    scores = jnp.where(allowed[None], scores, jnp.float32(-1e30))
    row_max = jnp.max(scores, axis=-1, keepdims=True)
    exp_scores = jnp.exp(scores - row_max)
    probs = (exp_scores / jnp.sum(exp_scores, axis=-1, keepdims=True)).astype(jnp.bfloat16)
    attended = jnp.einsum(
        "hqk,khd->qhd", probs, values_proj.reshape(head_shape), preferred_element_type=jnp.float32
    )
    attended = attended.astype(jnp.bfloat16).reshape(row_count, head_count * HD)
    partial_out = block_project(attended, o_full, o_rows)
    branch = lax.psum_scatter(
        partial_out.astype(jnp.bfloat16), "tensor", scatter_dimension=1, tiled=True
    ).astype(jnp.float32)
    return (u_half.astype(jnp.float32) + branch).astype(jnp.bfloat16)


def body(
    tokens,
    norm_gains,
    q_blocks,
    k_blocks,
    v_blocks,
    o_blocks,
    q_rows,
    k_rows,
    v_rows,
    o_rows,
    mask_blocks,
):
    sections = lax.axis_size("pipe")
    segment_idx = lax.axis_index("pipe")
    micro_count = mask_blocks.shape[0]
    seq_len = tokens.shape[0] // micro_count
    half_width = tokens.shape[1]
    q_full, k_full, v_full, o_all = (
        lax.all_gather(q_blocks, "fsdp", axis=3, tiled=True),
        lax.all_gather(k_blocks, "fsdp", axis=3, tiled=True),
        lax.all_gather(v_blocks, "fsdp", axis=3, tiled=True),
        lax.all_gather(o_blocks, "fsdp", axis=3, tiled=True),
    )

    def out_weights():
        return o_all[0]

    results = jnp.zeros((micro_count * seq_len, half_width), jnp.bfloat16)
    incoming = jnp.zeros((seq_len, half_width), jnp.bfloat16)
    total_steps = micro_count + sections - 1
    for step_idx in range(total_steps):
        if step_idx < micro_count:
            fresh_rows = tokens[step_idx * seq_len : (step_idx + 1) * seq_len]
        else:
            fresh_rows = jnp.zeros_like(incoming)
        u_half = jnp.where(segment_idx == 0, fresh_rows, incoming)
        offset = step_idx - segment_idx
        slot_idx = jnp.clip(offset, 0, micro_count - 1)
        mask_now = lax.dynamic_index_in_dim(mask_blocks, slot_idx, 0, keepdims=False)
        h_half = run_layer(
            u_half,
            mask_now,
            norm_gains[0],
            q_full[0],
            k_full[0],
            v_full[0],
            out_weights,
            q_rows[0],
            k_rows[0],
            v_rows[0],
            o_rows[0],
        )
        is_valid = (offset >= 0) & (offset < micro_count)
        row_start = slot_idx * seq_len
        current = lax.dynamic_slice_in_dim(results, row_start, seq_len, 0)
        results = lax.dynamic_update_slice_in_dim(
            results, jnp.where(is_valid, h_half, current), row_start, 0
        )
        if step_idx + 1 < total_steps:
            incoming = from_behind(h_half, "pipe", 1)
    return results[None]


def solution(mesh):
    placed = (
        P("fsdp", "tensor"),
        P("pipe", None),
        P("pipe", None, "tensor", "fsdp", None),
        P("pipe", None, "tensor", "fsdp", None),
        P("pipe", None, "tensor", "fsdp", None),
        P("pipe", "tensor", None, "fsdp", None),
        P("pipe", None, "tensor"),
        P("pipe", None, "tensor"),
        P("pipe", None, "tensor"),
        P("pipe", "tensor", None),
        P("fsdp", None, None),
    )
    return jax.shard_map(
        body, mesh=mesh, in_specs=placed, out_specs=P("pipe", "fsdp", "tensor"), check_vma=False
    )
```

profile of v0, /device:TPU:1, one launch (start us, length us, event | category | flops | bytes accessed | tf_op | source)
XLA Modules:
  0.0 690.7 jit_solution(11814978129373047153)
XLA Ops:
  11.5 7.5 %all_gather.30 = bf16[64,4096]{1,0:T(8,128)(2,1)S(1)} all-gather(bf16[64,2048]{1,0:T(8,128)(2,1)S(1)} %slice_select_fusion.2), channel_id=1, replica_groups=mesh['pipe'=4,'fsdp'=32,'tensor'=2] {'tensor'}, dimensions={1}, use_global_device_ids=true | all-gather | bytes 786432 | tf_op jit(solution)/shard_map/all_gather | solution.py:28
  23.5 77.3 %all-gather.7.cloned.1.call-done = bf16[1,4,8,256,256]{4,3,2,1,0:T(8,128)(2,1)} async-done(((bf16[1,4,8,8,256]{4,3,2,1,0:T(8,128)(2,1)}), bf16[1,4,8,256,256]{4,3,2,1,0:T(8,128)(2,1)}) %all-gather.7.cloned.1.call-update) | async-done | bytes 4194320 | tf_op jit(solution)/shard_map/all_gather | solution.py:80
  100.8 3.3 fusion.258
  104.4 82.5 %all-gather.9.cloned.1.call-done = bf16[1,4,8,256,256]{4,3,2,1,0:T(8,128)(2,1)} async-done(((bf16[1,4,8,8,256]{4,3,2,1,0:T(8,128)(2,1)}), bf16[1,4,8,256,256]{4,3,2,1,0:T(8,128)(2,1)}) %all-gather.9.cloned.1.call-update) | async-done | bytes 4194320 | tf_op jit(solution)/shard_map/all_gather | solution.py:81
  186.8 3.0 fusion.276
  190.1 82.8 %all-gather.5.cloned.1.call-done = bf16[1,4,8,256,256]{4,3,2,1,0:T(8,128)(2,1)} async-done(((bf16[1,4,8,8,256]{4,3,2,1,0:T(8,128)(2,1)}), bf16[1,4,8,256,256]{4,3,2,1,0:T(8,128)(2,1)}) %all-gather.5.cloned.1.call-update) | async-done | bytes 4194320 | tf_op jit(solution)/shard_map/all_gather | solution.py:82
  272.9 3.0 fusion.240
  277.8 80.9 %all-gather.11.cloned.1.call-done = bf16[1,2,16,256,256]{4,3,2,1,0:T(8,128)(2,1)} async-done(((bf16[1,2,16,8,256]{4,3,2,1,0:T(8,128)(2,1)}), bf16[1,2,16,256,256]{4,3,2,1,0:T(8,128)(2,1)}) %all-gather.11.cloned.1.call-update) | async-done | bytes 4194320 | tf_op jit(solution)/shard_map/all_gather | solution.py:83
  362.6 16.0 %reduce-scatter.7.cloned.1.call-done = bf16[64,2048]{1,0:T(8,128)(2,1)} async-done(((bf16[64,4096]{1,0:T(8,128)(2,1)}), bf16[64,2048]{1,0:T(8,128)(2,1)}) %reduce-scatter.7.cloned.1.call-update) | async-done | bytes 262160 | tf_op jit(solution)/shard_map/reduce_scatter | solution.py:55
  379.8 3.1 collective-permute-start
  383.2 4.5 collective-permute-done
  388.5 6.8 all_gather.35
  398.6 3.3 fusion.261
  402.9 3.0 fusion.279
  407.5 3.0 fusion.243
  412.1 3.0 fusion.105
  416.0 23.5 %reduce-scatter.9.cloned.1.call-done = bf16[64,2048]{1,0:T(8,128)(2,1)} async-done(((bf16[64,4096]{1,0:T(8,128)(2,1)}), bf16[64,2048]{1,0:T(8,128)(2,1)}) %reduce-scatter.9.cloned.1.call-update) | async-done | bytes 262160 | tf_op jit(solution)/shard_map/reduce_scatter | solution.py:55
  440.6 3.1 collective-permute-start.1
  444.0 4.5 collective-permute-done.1
  450.3 7.0 %all_gather.36 = bf16[64,4096]{1,0:T(8,128)(2,1)S(1)} all-gather(bf16[64,2048]{1,0:T(8,128)(2,1)S(1)} %slice_select_fusion), channel_id=1, replica_groups=mesh['pipe'=4,'fsdp'=32,'tensor'=2] {'tensor'}, dimensions={1}, use_global_device_ids=true | all-gather | bytes 786432 | tf_op jit(solution)/shard_map/all_gather | solution.py:28
  460.6 3.3 fusion.264
  469.5 3.0 fusion.246
  474.1 3.0 fusion.108
  478.0 23.5 %reduce-scatter.11.cloned.1.call-done = bf16[64,2048]{1,0:T(8,128)(2,1)} async-done(((bf16[64,4096]{1,0:T(8,128)(2,1)}), bf16[64,2048]{1,0:T(8,128)(2,1)}) %reduce-scatter.11.cloned.1.call-update) | async-done | bytes 262160 | tf_op jit(solution)/shard_map/reduce_scatter | solution.py:55
  502.6 3.1 collective-permute-start.2
  506.0 4.5 collective-permute-done.2
  510.6 6.9 all_gather.37
  520.7 3.3 fusion.267
  525.0 3.0 fusion.285
  529.7 3.0 fusion.249
  534.2 3.0 fusion.111
  538.2 23.4 %reduce-scatter.13.cloned.1.call-done = bf16[64,2048]{1,0:T(8,128)(2,1)} async-done(((bf16[64,4096]{1,0:T(8,128)(2,1)}), bf16[64,2048]{1,0:T(8,128)(2,1)}) %reduce-scatter.13.cloned.1.call-update) | async-done | bytes 262160 | tf_op jit(solution)/shard_map/reduce_scatter | solution.py:55
  562.7 3.1 collective-permute-start.3
  566.1 4.5 collective-permute-done.3
  570.6 7.0 %all_gather.38 = bf16[64,4096]{1,0:T(8,128)(2,1)S(1)} all-gather(bf16[64,2048]{1,0:T(8,128)(2,1)S(1)} %broadcast_select_fusion.1), channel_id=1, replica_groups=mesh['pipe'=4,'fsdp'=32,'tensor'=2] {'tensor'}, dimensions={1}, use_global_device_ids=true | all-gather | bytes 786432 | tf_op jit(solution)/shard_map/all_gather | solution.py:28
  581.0 3.3 fusion.270
  585.3 3.0 fusion.288
  589.9 3.0 fusion.252
  594.5 3.0 fusion.114
  598.4 23.6 %reduce-scatter.15.cloned.1.call-done = bf16[64,2048]{1,0:T(8,128)(2,1)} async-done(((bf16[64,4096]{1,0:T(8,128)(2,1)}), bf16[64,2048]{1,0:T(8,128)(2,1)}) %reduce-scatter.15.cloned.1.call-update) | async-done | bytes 262160 | tf_op jit(solution)/shard_map/reduce_scatter | solution.py:55
  623.1 3.1 collective-permute-start.4
  626.5 4.5 collective-permute-done.4
  631.0 6.8 all_gather.39
  641.2 3.3 fusion.273
  645.5 3.0 fusion.291
  650.1 3.0 fusion.255
  654.7 3.0 fusion.117
  659.4 22.6 %reduce-scatter.17.cloned.1.call-done = bf16[64,2048]{1,0:T(8,128)(2,1)} async-done(((bf16[64,4096]{1,0:T(8,128)(2,1)}), bf16[64,2048]{1,0:T(8,128)(2,1)}) %reduce-scatter.17.cloned.1.call-update) | async-done | bytes 262160 | tf_op jit(solution)/shard_map/reduce_scatter | solution.py:55
  (230 shorter events, 71.6 us)
Async XLA Ops:
  6.5 13.6 %copy-start.14 = (s32[1,4,8]{2,1,0:T(4,128)S(1)}, s32[1,4,8]{2,1,0:T(4,128)}, u32[]{:S(2)}) copy-start(s32[1,4,8]{2,1,0:T(4,128)} %param.17) | copy-start | bytes 388
  6.5 13.6 %copy-start.13 = (s32[1,4,8]{2,1,0:T(4,128)S(1)}, s32[1,4,8]{2,1,0:T(4,128)}, u32[]{:S(2)}) copy-start(s32[1,4,8]{2,1,0:T(4,128)} %param.18) | copy-start | bytes 388
  6.5 94.2 %all-gather.7.cloned.1.call-start = ((), (), s32[]{:S(2)}) async-start(), calls=%async_computation.7 | async-start | bytes 4325376 | tf_op jit(solution)/shard_map/all_gather | solution.py:80
  7.3 179.6 %all-gather.9.cloned.1.call-start = ((), (), s32[]{:S(2)}) async-start(), calls=%async_computation.8 | async-start | bytes 4325376 | tf_op jit(solution)/shard_map/all_gather | solution.py:81
  8.0 264.8 %all-gather.5.cloned.1.call-start = ((), (), s32[]{:S(2)}) async-start(), calls=%async_computation.6 | async-start | bytes 4325376 | tf_op jit(solution)/shard_map/all_gather | solution.py:82
  8.7 13.9 %copy-start.12 = (s32[1,4,8]{2,1,0:T(4,128)S(1)}, s32[1,4,8]{2,1,0:T(4,128)}, u32[]{:S(2)}) copy-start(s32[1,4,8]{2,1,0:T(4,128)} %param.19) | copy-start | bytes 388
  8.8 350.0 %all-gather.11.cloned.1.call-start = ((), (), s32[]{:S(2)}) async-start(), calls=%async_computation.9 | async-start | bytes 4325376 | tf_op jit(solution)/shard_map/all_gather | solution.py:83
  9.3 369.3 %reduce-scatter.7.cloned.1.call-start = ((), (), s32[]{:S(2)}) async-start(), calls=%async_computation.10 | async-start | bytes 786432 | tf_op jit(solution)/shard_map/reduce_scatter | solution.py:55
  19.2 4.2 copy-start.15
  277.8 100.9 %copy-start.4 = (bf16[192,2048]{1,0:T(8,128)(2,1)S(1)}, bf16[192,2048]{1,0:T(8,128)(2,1)}, u32[]{:S(2)}) copy-start(bf16[192,2048]{1,0:T(8,128)(2,1)} %param.11) | copy-start | bytes 2359300
  361.7 33.8 %copy-start.11 = (f32[1,4096]{1,0:T(1,128)S(1)}, f32[1,4096]{1,0:T(1,128)}, u32[]{:S(2)}) copy-start(f32[1,4096]{1,0:T(1,128)} %param.12) | copy-start | bytes 49156
  362.6 76.9 %reduce-scatter.9.cloned.1.call-start = ((), (), s32[]{:S(2)}) async-start(), calls=%async_computation.11 | async-start | bytes 786432 | tf_op jit(solution)/shard_map/reduce_scatter | solution.py:55
  379.8 7.9 %collective-permute-start = (bf16[64,2048]{1,0:T(8,128)(2,1)S(1)}, bf16[64,2048]{1,0:T(8,128)(2,1)S(1)}, u32[]{:S(2)}, u32[]{:S(2)}) collective-permute-start(bf16[64,2048]{1,0:T(8,128)(2,1)S(1)} %get-tuple-element.14), channel_id=1, source_target_pairs={{0,64},{64,128},{128,192},{1,65},{65,129},{129,193},{2,66},{66,130... | collective-permute-start | bytes 786440 | tf_op jit(solution)/shard_map/ppermute | solution.py:13
  387.8 0.7 copy-start
  412.1 27.4 %copy-start.1 = (bf16[64,2048]{1,0:T(8,128)(2,1)S(1)}, bf16[64,2048]{1,0:T(8,128)(2,1)}, u32[]{:S(2)}) copy-start(bf16[64,2048]{1,0:T(8,128)(2,1)} %copy-done) | copy-start | bytes 786436
  416.0 85.5 %reduce-scatter.11.cloned.1.call-start = ((), (), s32[]{:S(2)}) async-start(), calls=%async_computation.12 | async-start | bytes 786432 | tf_op jit(solution)/shard_map/reduce_scatter | solution.py:55
  440.6 7.9 %collective-permute-start.1 = (bf16[64,2048]{1,0:T(8,128)(2,1)S(1)}, bf16[64,2048]{1,0:T(8,128)(2,1)S(1)}, u32[]{:S(2)}, u32[]{:S(2)}) collective-permute-start(bf16[64,2048]{1,0:T(8,128)(2,1)S(1)} %get-tuple-element.12), channel_id=1, source_target_pairs={{0,64},{64,128},{128,192},{1,65},{65,129},{129,193},{2,66},{66,130... | collective-permute-start | bytes 786440 | tf_op jit(solution)/shard_map/ppermute | solution.py:13
  449.5 0.7 copy-start.2
  474.1 27.4 %copy-start.3 = (bf16[64,2048]{1,0:T(8,128)(2,1)S(1)}, bf16[64,2048]{1,0:T(8,128)(2,1)}, u32[]{:S(2)}) copy-start(bf16[64,2048]{1,0:T(8,128)(2,1)} %copy-done.2) | copy-start | bytes 786436
  477.9 83.7 %reduce-scatter.13.cloned.1.call-start = ((), (), s32[]{:S(2)}) async-start(), calls=%async_computation.13 | async-start | bytes 786432 | tf_op jit(solution)/shard_map/reduce_scatter | solution.py:55
  502.6 8.0 %collective-permute-start.2 = (bf16[64,2048]{1,0:T(8,128)(2,1)S(1)}, bf16[64,2048]{1,0:T(8,128)(2,1)S(1)}, u32[]{:S(2)}, u32[]{:S(2)}) collective-permute-start(bf16[64,2048]{1,0:T(8,128)(2,1)S(1)} %get-tuple-element.10), channel_id=1, source_target_pairs={{0,64},{64,128},{128,192},{1,65},{65,129},{129,193},{2,66},{66,130... | collective-permute-start | bytes 786440 | tf_op jit(solution)/shard_map/ppermute | solution.py:13
  510.5 7.3 %copy-start.7 = (bf16[64,2048]{1,0:T(8,128)(2,1)}, bf16[64,2048]{1,0:T(8,128)(2,1)S(1)}, u32[]{:S(2)}) copy-start(bf16[64,2048]{1,0:T(8,128)(2,1)S(1)} %collective-permute-done.2) | copy-start | bytes 786436
  534.2 27.4 %copy-start.8 = (bf16[64,2048]{1,0:T(8,128)(2,1)S(1)}, bf16[64,2048]{1,0:T(8,128)(2,1)}, u32[]{:S(2)}) copy-start(bf16[64,2048]{1,0:T(8,128)(2,1)} %copy-done.7) | copy-start | bytes 786436
  538.1 83.9 %reduce-scatter.15.cloned.1.call-start = ((), (), s32[]{:S(2)}) async-start(), calls=%async_computation.14 | async-start | bytes 786432 | tf_op jit(solution)/shard_map/reduce_scatter | solution.py:55
  562.7 7.9 %collective-permute-start.3 = (bf16[64,2048]{1,0:T(8,128)(2,1)S(1)}, bf16[64,2048]{1,0:T(8,128)(2,1)S(1)}, u32[]{:S(2)}, u32[]{:S(2)}) collective-permute-start(bf16[64,2048]{1,0:T(8,128)(2,1)S(1)} %get-tuple-element.8), channel_id=1, source_target_pairs={{0,64},{64,128},{128,192},{1,65},{65,129},{129,193},{2,66},{66,130... | collective-permute-start | bytes 786440 | tf_op jit(solution)/shard_map/ppermute | solution.py:13
  570.6 7.5 %copy-start.9 = (bf16[64,2048]{1,0:T(8,128)(2,1)}, bf16[64,2048]{1,0:T(8,128)(2,1)S(1)}, u32[]{:S(2)}) copy-start(bf16[64,2048]{1,0:T(8,128)(2,1)S(1)} %collective-permute-done.3) | copy-start | bytes 786436
  594.5 27.5 %copy-start.10 = (bf16[64,2048]{1,0:T(8,128)(2,1)S(1)}, bf16[64,2048]{1,0:T(8,128)(2,1)}, u32[]{:S(2)}) copy-start(bf16[64,2048]{1,0:T(8,128)(2,1)} %copy-done.9) | copy-start | bytes 786436
  598.4 83.7 %reduce-scatter.17.cloned.1.call-start = ((), (), s32[]{:S(2)}) async-start(), calls=%async_computation.15 | async-start | bytes 786432 | tf_op jit(solution)/shard_map/reduce_scatter | solution.py:55
  623.1 7.9 %collective-permute-start.4 = (bf16[64,2048]{1,0:T(8,128)(2,1)S(1)}, bf16[64,2048]{1,0:T(8,128)(2,1)S(1)}, u32[]{:S(2)}, u32[]{:S(2)}) collective-permute-start(bf16[64,2048]{1,0:T(8,128)(2,1)S(1)} %get-tuple-element.6), channel_id=1, source_target_pairs={{0,64},{64,128},{128,192},{1,65},{65,129},{129,193},{2,66},{66,130... | collective-permute-start | bytes 786440 | tf_op jit(solution)/shard_map/ppermute | solution.py:13
  631.0 7.3 %copy-start.5 = (bf16[64,2048]{1,0:T(8,128)(2,1)}, bf16[64,2048]{1,0:T(8,128)(2,1)S(1)}, u32[]{:S(2)}) copy-start(bf16[64,2048]{1,0:T(8,128)(2,1)S(1)} %collective-permute-done.4) | copy-start | bytes 786436
  654.7 27.4 %copy-start.6 = (bf16[64,2048]{1,0:T(8,128)(2,1)S(1)}, bf16[64,2048]{1,0:T(8,128)(2,1)}, u32[]{:S(2)}) copy-start(bf16[64,2048]{1,0:T(8,128)(2,1)} %copy-done.5) | copy-start | bytes 786436
Sparse Core Ops, SparseCore 0:
  9.9 90.8 all-gather.6
  103.3 83.4 all-gather.8
  189.4 83.4 all-gather.4
  275.3 83.4 all-gather.10
  362.7 15.8 reduce-scatter.6
  416.1 23.3 reduce-scatter.8
  478.1 23.3 reduce-scatter.10
  538.2 23.3 reduce-scatter.12
  598.5 23.4 reduce-scatter.14
  658.7 23.3 reduce-scatter.16
where the time goes:
time: 692 us; the launch traced here: 691 us
  waiting for transfers between devices  481 us (70%)
  matrix products  82.2 us (12%)
  blocking collectives  42 us (6%)
  local copies, waits for them, and re-layouts  40.1 us (6%)
  starting transfers between devices  16 us (2%)
  between operations  14.9 us (2%)
  other arithmetic  14.1 us (2%)
    reduce_scatter x6, waiting for transfers between devices, run_layer(): lax.psum_scatter(partial_out.astype(jnp.bfloat16), 'tensor', scatter_dime...  133 us
    all_gather x1, waiting for transfers between devices, body(): lax.all_gather(v_blocks, 'fsdp', axis=3, tiled=True)  82.8 us
    all_gather x1, waiting for transfers between devices, body(): lax.all_gather(k_blocks, 'fsdp', axis=3, tiled=True)  82.5 us
    all_gather x1, waiting for transfers between devices, body(): lax.all_gather(o_blocks, 'fsdp', axis=3, tiled=True)  80.9 us
    all_gather x1, waiting for transfers between devices, body(): lax.all_gather(q_blocks, 'fsdp', axis=3, tiled=True)  77.3 us
    dot_general x24, matrix products, block_project(): jnp.einsum('rpcb,pcbe->rce', picked, blocks, preferred_element_type=jnp.f...  73.8 us
    all_gather x6, blocking collectives, run_layer(): gathered = lax.all_gather(u_half, 'tensor', axis=1, tiled=True)  42 us
    ppermute x5, waiting for transfers between devices, from_behind(): lax.ppermute(value, axis, [(source, source + steps) for source in range(i...  22.6 us
  transfers between devices with their start and end apart: 15, of which 15 were waited for; matrix products, arithmetic and copies ran while one was open for 3% of the time, Pallas kernels for 0%

commit v1 on v0

--- a/solution.py
+++ b/solution.py
@@ -79,7 +79,9 @@
     q_full, k_full, v_full, o_all = (
         lax.all_gather(q_blocks, "fsdp", axis=3, tiled=True),
         lax.all_gather(k_blocks, "fsdp", axis=3, tiled=True),
-        lax.all_gather(v_blocks, "fsdp", axis=3, tiled=True),
+        jnp.concatenate(
+            lax.all_to_all(jnp.stack([v_blocks] * lax.axis_size("fsdp")), "fsdp", 0, 0), axis=3
+        ),
         lax.all_gather(o_blocks, "fsdp", axis=3, tiled=True),
     )
 

time: 692 us -> 649 us (0.938)
  waiting for transfers between devices: 481 us -> 415 us
  starting transfers between devices: 16 us -> 28.9 us
  blocking collectives: 42 us -> 52.6 us
    all_gather x1 -> x0, waiting for transfers between devices: 82.8 us -> none  [body(): lax.all_gather(v_blocks, 'fsdp', axis=3, tiled=True)]
    all_gather x1, waiting for transfers between devices: 77.3 us -> 96 us  [body(): lax.all_gather(q_blocks, 'fsdp', axis=3, tiled=True)]
    all_to_all x0 -> x1, starting transfers between devices: none -> 12.8 us  [body(): lax.all_to_all(jnp.stack([v_blocks] * lax.axis_size('fsdp')), 'fsdp', 0, 0)]
    all_gather x6, blocking collectives: 42 us -> 52.6 us  [run_layer(): gathered = lax.all_gather(u_half, 'tensor', axis=1, tiled=True)]
  transfers between devices with their start and end apart: 15 -> 15, of which waited for: 15 -> 14; matrix products, arithmetic and copies ran while one was open for 3% -> 3% of each run, Pallas kernels for 0% -> 0%
where the time goes in v1:
time: 649 us; the launch traced here: 647 us
  waiting for transfers between devices  415 us (64%)
  matrix products  80.9 us (12%)
  blocking collectives  52.6 us (8%)
  local copies, waits for them, and re-layouts  44.2 us (7%)
  starting transfers between devices  28.9 us (4%)
  between operations  14.6 us (2%)
  other arithmetic  11.6 us (2%)
    reduce_scatter x6, waiting for transfers between devices, run_layer(): lax.psum_scatter(partial_out.astype(jnp.bfloat16), 'tensor', scatter_dime...  133 us
    all_gather x1, waiting for transfers between devices, body(): lax.all_gather(q_blocks, 'fsdp', axis=3, tiled=True)  96 us
    all_gather x1, waiting for transfers between devices, body(): lax.all_gather(k_blocks, 'fsdp', axis=3, tiled=True)  83.7 us
    all_gather x1, waiting for transfers between devices, body(): lax.all_gather(o_blocks, 'fsdp', axis=3, tiled=True)  77.7 us
    dot_general x24, matrix products, block_project(): jnp.einsum('rpcb,pcbe->rce', picked, blocks, preferred_element_type=jnp.f...  72.5 us
    all_gather x6, blocking collectives, run_layer(): gathered = lax.all_gather(u_half, 'tensor', axis=1, tiled=True)  52.6 us
    ppermute x5, waiting for transfers between devices, from_behind(): lax.ppermute(value, axis, [(source, source + steps) for source in range(i...  22.4 us
    gather x24, local copies, waits for them, and re-layouts, block_project(): picked = row_blocks[:, pattern]  20.7 us
  transfers between devices with their start and end apart: 15, of which 14 were waited for; matrix products, arithmetic and copies ran while one was open for 3% of the time, Pallas kernels for 0%

profile of v1, /device:TPU:1, one launch (start us, length us, event | category | flops | bytes accessed | tf_op | source)
XLA Modules:
  0.0 647.4 jit_solution(1813750320073196486)
XLA Ops:
  8.0 3.4 stack.2
  11.4 12.8 %all-to-all-start = ((bf16[32,1,4,8,8,256]{5,4,3,2,1,0:T(8,128)(2,1)}), bf16[32,1,4,8,8,256]{5,4,3,2,1,0:T(8,128)(2,1)}, u32[]{:S(2)}, u32[]{:S(2)}) async-start(bf16[32,1,4,8,8,256]{5,4,3,2,1,0:T(8,128)(2,1)} %stack.2), calls=%async_computation | async-start | bytes 8388608 | tf_op jit(solution)/shard_map/all_to_all | solution.py:83
  25.3 18.2 %all_gather.27 = bf16[64,4096]{1,0:T(8,128)(2,1)S(1)} all-gather(bf16[64,2048]{1,0:T(8,128)(2,1)S(1)} %slice_select_fusion.2), channel_id=1, replica_groups=mesh['pipe'=4,'fsdp'=32,'tensor'=2] {'tensor'}, dimensions={1}, use_global_device_ids=true | all-gather | bytes 786432 | tf_op jit(solution)/shard_map/all_gather | solution.py:28
  47.3 96.0 %all-gather.4.cloned.1.call-done = bf16[1,4,8,256,256]{4,3,2,1,0:T(8,128)(2,1)} async-done(((bf16[1,4,8,8,256]{4,3,2,1,0:T(8,128)(2,1)}), bf16[1,4,8,256,256]{4,3,2,1,0:T(8,128)(2,1)}) %all-gather.4.cloned.1.call-update) | async-done | bytes 4194320 | tf_op jit(solution)/shard_map/all_gather | solution.py:80
  147.2 83.7 %all-gather.6.cloned.1.call-done = bf16[1,4,8,256,256]{4,3,2,1,0:T(8,128)(2,1)} async-done(((bf16[1,4,8,8,256]{4,3,2,1,0:T(8,128)(2,1)}), bf16[1,4,8,256,256]{4,3,2,1,0:T(8,128)(2,1)}) %all-gather.6.cloned.1.call-update) | async-done | bytes 4194320 | tf_op jit(solution)/shard_map/all_gather | solution.py:81
  230.9 3.0 fusion.282
  234.2 3.0 fusion.246
  239.3 77.7 %all-gather.8.cloned.1.call-done = bf16[1,2,16,256,256]{4,3,2,1,0:T(8,128)(2,1)} async-done(((bf16[1,2,16,8,256]{4,3,2,1,0:T(8,128)(2,1)}), bf16[1,2,16,256,256]{4,3,2,1,0:T(8,128)(2,1)}) %all-gather.8.cloned.1.call-update) | async-done | bytes 4194320 | tf_op jit(solution)/shard_map/all_gather | solution.py:85
  320.9 16.0 %reduce-scatter.7.cloned.1.call-done = bf16[64,2048]{1,0:T(8,128)(2,1)} async-done(((bf16[64,4096]{1,0:T(8,128)(2,1)}), bf16[64,2048]{1,0:T(8,128)(2,1)}) %reduce-scatter.7.cloned.1.call-update) | async-done | bytes 262160 | tf_op jit(solution)/shard_map/reduce_scatter | solution.py:55
  338.0 3.1 collective-permute-start
  341.4 4.5 collective-permute-done
  346.7 6.8 %all_gather.31 = bf16[64,4096]{1,0:T(8,128)(2,1)S(1)} all-gather(bf16[64,2048]{1,0:T(8,128)(2,1)S(1)} %slice_select_fusion.1), channel_id=1, replica_groups=mesh['pipe'=4,'fsdp'=32,'tensor'=2] {'tensor'}, dimensions={1}, use_global_device_ids=true | all-gather | bytes 786432 | tf_op jit(solution)/shard_map/all_gather | solution.py:28
  356.8 3.0 fusion.267
  360.8 3.1 fusion.285
  365.5 3.0 fusion.249
  370.1 3.0 fusion.129
  374.0 23.5 %reduce-scatter.9.cloned.1.call-done = bf16[64,2048]{1,0:T(8,128)(2,1)} async-done(((bf16[64,4096]{1,0:T(8,128)(2,1)}), bf16[64,2048]{1,0:T(8,128)(2,1)}) %reduce-scatter.9.cloned.1.call-update) | async-done | bytes 262160 | tf_op jit(solution)/shard_map/reduce_scatter | solution.py:55
  398.6 3.3 collective-permute-start.1
  402.2 4.3 collective-permute-done.1
  408.3 6.8 %all_gather.32 = bf16[64,4096]{1,0:T(8,128)(2,1)S(1)} all-gather(bf16[64,2048]{1,0:T(8,128)(2,1)S(1)} %slice_select_fusion), channel_id=1, replica_groups=mesh['pipe'=4,'fsdp'=32,'tensor'=2] {'tensor'}, dimensions={1}, use_global_device_ids=true | all-gather | bytes 786432 | tf_op jit(solution)/shard_map/all_gather | solution.py:28
  418.4 3.0 fusion.270
  422.4 3.1 fusion.288
  427.1 3.0 fusion.252
  431.7 3.0 fusion.132
  435.6 23.5 %reduce-scatter.11.cloned.1.call-done = bf16[64,2048]{1,0:T(8,128)(2,1)} async-done(((bf16[64,4096]{1,0:T(8,128)(2,1)}), bf16[64,2048]{1,0:T(8,128)(2,1)}) %reduce-scatter.11.cloned.1.call-update) | async-done | bytes 262160 | tf_op jit(solution)/shard_map/reduce_scatter | solution.py:55
  460.2 3.1 collective-permute-start.2
  463.6 4.5 collective-permute-done.2
  468.2 6.8 %all_gather.33 = bf16[64,4096]{1,0:T(8,128)(2,1)S(1)} all-gather(bf16[64,2048]{1,0:T(8,128)(2,1)S(1)} %broadcast_select_fusion.2), channel_id=1, replica_groups=mesh['pipe'=4,'fsdp'=32,'tensor'=2] {'tensor'}, dimensions={1}, use_global_device_ids=true | all-gather | bytes 786432 | tf_op jit(solution)/shard_map/all_gather | solution.py:28
  482.3 3.1 fusion.291
  487.0 3.0 fusion.255
  491.6 3.0 fusion.135
  495.5 23.5 %reduce-scatter.13.cloned.1.call-done = bf16[64,2048]{1,0:T(8,128)(2,1)} async-done(((bf16[64,4096]{1,0:T(8,128)(2,1)}), bf16[64,2048]{1,0:T(8,128)(2,1)}) %reduce-scatter.13.cloned.1.call-update) | async-done | bytes 262160 | tf_op jit(solution)/shard_map/reduce_scatter | solution.py:55
  520.1 3.1 collective-permute-start.3
  523.5 4.5 collective-permute-done.3
  528.1 7.1 %all_gather.34 = bf16[64,4096]{1,0:T(8,128)(2,1)S(1)} all-gather(bf16[64,2048]{1,0:T(8,128)(2,1)S(1)} %broadcast_select_fusion.1), channel_id=1, replica_groups=mesh['pipe'=4,'fsdp'=32,'tensor'=2] {'tensor'}, dimensions={1}, use_global_device_ids=true | all-gather | bytes 786432 | tf_op jit(solution)/shard_map/all_gather | solution.py:28
  538.5 3.0 fusion.276
  542.5 3.1 fusion.294
  547.2 3.0 fusion.258
  551.8 3.0 fusion.138
  555.7 23.5 %reduce-scatter.15.cloned.1.call-done = bf16[64,2048]{1,0:T(8,128)(2,1)} async-done(((bf16[64,4096]{1,0:T(8,128)(2,1)}), bf16[64,2048]{1,0:T(8,128)(2,1)}) %reduce-scatter.15.cloned.1.call-update) | async-done | bytes 262160 | tf_op jit(solution)/shard_map/reduce_scatter | solution.py:55
  580.3 3.1 collective-permute-start.4
  583.7 4.5 collective-permute-done.4
  588.3 6.8 %all_gather.35 = bf16[64,4096]{1,0:T(8,128)(2,1)S(1)} all-gather(bf16[64,2048]{1,0:T(8,128)(2,1)S(1)} %broadcast_select_fusion), channel_id=1, replica_groups=mesh['pipe'=4,'fsdp'=32,'tensor'=2] {'tensor'}, dimensions={1}, use_global_device_ids=true | all-gather | bytes 786432 | tf_op jit(solution)/shard_map/all_gather | solution.py:28
  598.4 3.0 fusion.279
  602.4 3.1 fusion.297
  607.1 3.0 fusion.261
  611.7 3.0 fusion.141
  616.5 22.6 %reduce-scatter.17.cloned.1.call-done = bf16[64,2048]{1,0:T(8,128)(2,1)} async-done(((bf16[64,4096]{1,0:T(8,128)(2,1)}), bf16[64,2048]{1,0:T(8,128)(2,1)}) %reduce-scatter.17.cloned.1.call-update) | async-done | bytes 262160 | tf_op jit(solution)/shard_map/reduce_scatter | solution.py:55
  (246 shorter events, 72.2 us)
Async XLA Ops:
  6.5 136.7 %all-gather.4.cloned.1.call-start = ((), (), s32[]{:S(2)}) async-start(), calls=%async_computation.7 | async-start | bytes 4325376 | tf_op jit(solution)/shard_map/all_gather | solution.py:80
  7.3 223.7 %all-gather.6.cloned.1.call-start = ((), (), s32[]{:S(2)}) async-start(), calls=%async_computation.8 | async-start | bytes 4325376 | tf_op jit(solution)/shard_map/all_gather | solution.py:81
  11.4 13.6 %copy-start.19 = (s32[3,4,4]{2,1,0:T(4,128)S(1)}, s32[3,4,4]{2,1,0:T(4,128)}, u32[]{:S(2)}) copy-start(s32[3,4,4]{2,1,0:T(4,128)} %param.21) | copy-start | bytes 580
  11.4 13.9 %copy-start.4 = (bf16[192,2048]{1,0:T(8,128)(2,1)S(1)}, bf16[192,2048]{1,0:T(8,128)(2,1)}, u32[]{:S(2)}) copy-start(bf16[192,2048]{1,0:T(8,128)(2,1)} %param.11) | copy-start | bytes 2359300
  11.4 32.4 %copy-start.17 = (f32[1,4096]{1,0:T(1,128)S(1)}, f32[1,4096]{1,0:T(1,128)}, u32[]{:S(2)}) copy-start(f32[1,4096]{1,0:T(1,128)} %param.12) | copy-start | bytes 49156
  11.4 32.7 %copy-start.21 = (s32[1,4,8]{2,1,0:T(4,128)S(1)}, s32[1,4,8]{2,1,0:T(4,128)}, u32[]{:S(2)}) copy-start(s32[1,4,8]{2,1,0:T(4,128)} %param.18) | copy-start | bytes 388
  11.4 32.7 %copy-start.22 = (s32[1,4,8]{2,1,0:T(4,128)S(1)}, s32[1,4,8]{2,1,0:T(4,128)}, u32[]{:S(2)}) copy-start(s32[1,4,8]{2,1,0:T(4,128)} %param.17) | copy-start | bytes 388
  11.4 222.8 %all-to-all-start = ((bf16[32,1,4,8,8,256]{5,4,3,2,1,0:T(8,128)(2,1)}), bf16[32,1,4,8,8,256]{5,4,3,2,1,0:T(8,128)(2,1)}, u32[]{:S(2)}, u32[]{:S(2)}) async-start(bf16[32,1,4,8,8,256]{5,4,3,2,1,0:T(8,128)(2,1)} %stack.2), calls=%async_computation | async-start | bytes 8388608 | tf_op jit(solution)/shard_map/all_to_all | solution.py:83
  24.2 21.3 %copy-start.20 = (s32[1,4,8]{2,1,0:T(4,128)S(1)}, s32[1,4,8]{2,1,0:T(4,128)}, u32[]{:S(2)}) copy-start(s32[1,4,8]{2,1,0:T(4,128)} %param.19) | copy-start | bytes 388
  24.2 292.8 %all-gather.8.cloned.1.call-start = ((), (), s32[]{:S(2)}) async-start(), calls=%async_computation.9 | async-start | bytes 4325376 | tf_op jit(solution)/shard_map/all_gather | solution.py:85
  24.9 311.9 %reduce-scatter.7.cloned.1.call-start = ((), (), s32[]{:S(2)}) async-start(), calls=%async_computation.10 | async-start | bytes 786432 | tf_op jit(solution)/shard_map/reduce_scatter | solution.py:55
  43.8 3.4 copy-start.23
  146.3 87.9 %copy-start.7 = (bf16[32,64,256]{2,1,0:T(8,128)(2,1)S(1)}, bf16[32,64,256]{2,1,0:T(8,128)(2,1)}, u32[]{:S(2)}) copy-start(bf16[32,64,256]{2,1,0:T(8,128)(2,1)} %gather_fusion) | copy-start | bytes 3145732
  233.9 3.6 copy-start.18
  320.8 76.7 %reduce-scatter.9.cloned.1.call-start = ((), (), s32[]{:S(2)}) async-start(), calls=%async_computation.11 | async-start | bytes 786432 | tf_op jit(solution)/shard_map/reduce_scatter | solution.py:55
  338.0 7.9 %collective-permute-start = (bf16[64,2048]{1,0:T(8,128)(2,1)S(1)}, bf16[64,2048]{1,0:T(8,128)(2,1)S(1)}, u32[]{:S(2)}, u32[]{:S(2)}) collective-permute-start(bf16[64,2048]{1,0:T(8,128)(2,1)S(1)} %get-tuple-element.14), channel_id=1, source_target_pairs={{0,64},{64,128},{128,192},{1,65},{65,129},{129,193},{2,66},{66,130... | collective-permute-start | bytes 786440 | tf_op jit(solution)/shard_map/ppermute | solution.py:13
  346.0 0.7 copy-start
  360.8 4.7 copy-start.9
  370.1 27.4 %copy-start.1 = (bf16[64,2048]{1,0:T(8,128)(2,1)S(1)}, bf16[64,2048]{1,0:T(8,128)(2,1)}, u32[]{:S(2)}) copy-start(bf16[64,2048]{1,0:T(8,128)(2,1)} %copy-done) | copy-start | bytes 786436
  374.0 85.2 %reduce-scatter.11.cloned.1.call-start = ((), (), s32[]{:S(2)}) async-start(), calls=%async_computation.12 | async-start | bytes 786432 | tf_op jit(solution)/shard_map/reduce_scatter | solution.py:55
  398.6 7.9 %collective-permute-start.1 = (bf16[64,2048]{1,0:T(8,128)(2,1)S(1)}, bf16[64,2048]{1,0:T(8,128)(2,1)S(1)}, u32[]{:S(2)}, u32[]{:S(2)}) collective-permute-start(bf16[64,2048]{1,0:T(8,128)(2,1)S(1)} %get-tuple-element.12), channel_id=1, source_target_pairs={{0,64},{64,128},{128,192},{1,65},{65,129},{129,193},{2,66},{66,130... | collective-permute-start | bytes 786440 | tf_op jit(solution)/shard_map/ppermute | solution.py:13
  407.5 0.7 copy-start.2
  422.4 4.7 copy-start.10
  431.7 27.4 %copy-start.3 = (bf16[64,2048]{1,0:T(8,128)(2,1)S(1)}, bf16[64,2048]{1,0:T(8,128)(2,1)}, u32[]{:S(2)}) copy-start(bf16[64,2048]{1,0:T(8,128)(2,1)} %copy-done.2) | copy-start | bytes 786436
  435.6 83.4 %reduce-scatter.13.cloned.1.call-start = ((), (), s32[]{:S(2)}) async-start(), calls=%async_computation.13 | async-start | bytes 786432 | tf_op jit(solution)/shard_map/reduce_scatter | solution.py:55
  460.2 7.9 %collective-permute-start.2 = (bf16[64,2048]{1,0:T(8,128)(2,1)S(1)}, bf16[64,2048]{1,0:T(8,128)(2,1)S(1)}, u32[]{:S(2)}, u32[]{:S(2)}) collective-permute-start(bf16[64,2048]{1,0:T(8,128)(2,1)S(1)} %get-tuple-element.10), channel_id=1, source_target_pairs={{0,64},{64,128},{128,192},{1,65},{65,129},{129,193},{2,66},{66,130... | collective-permute-start | bytes 786440 | tf_op jit(solution)/shard_map/ppermute | solution.py:13
  468.1 7.3 %copy-start.13 = (bf16[64,2048]{1,0:T(8,128)(2,1)}, bf16[64,2048]{1,0:T(8,128)(2,1)S(1)}, u32[]{:S(2)}) copy-start(bf16[64,2048]{1,0:T(8,128)(2,1)S(1)} %collective-permute-done.2) | copy-start | bytes 786436
  482.3 4.7 copy-start.11
  491.6 27.4 %copy-start.14 = (bf16[64,2048]{1,0:T(8,128)(2,1)S(1)}, bf16[64,2048]{1,0:T(8,128)(2,1)}, u32[]{:S(2)}) copy-start(bf16[64,2048]{1,0:T(8,128)(2,1)} %copy-done.13) | copy-start | bytes 786436
  495.5 83.7 %reduce-scatter.15.cloned.1.call-start = ((), (), s32[]{:S(2)}) async-start(), calls=%async_computation.14 | async-start | bytes 786432 | tf_op jit(solution)/shard_map/reduce_scatter | solution.py:55
  520.1 8.0 %collective-permute-start.3 = (bf16[64,2048]{1,0:T(8,128)(2,1)S(1)}, bf16[64,2048]{1,0:T(8,128)(2,1)S(1)}, u32[]{:S(2)}, u32[]{:S(2)}) collective-permute-start(bf16[64,2048]{1,0:T(8,128)(2,1)S(1)} %get-tuple-element.8), channel_id=1, source_target_pairs={{0,64},{64,128},{128,192},{1,65},{65,129},{129,193},{2,66},{66,130... | collective-permute-start | bytes 786440 | tf_op jit(solution)/shard_map/ppermute | solution.py:13
  528.1 7.5 %copy-start.15 = (bf16[64,2048]{1,0:T(8,128)(2,1)}, bf16[64,2048]{1,0:T(8,128)(2,1)S(1)}, u32[]{:S(2)}) copy-start(bf16[64,2048]{1,0:T(8,128)(2,1)S(1)} %collective-permute-done.3) | copy-start | bytes 786436
  542.5 4.7 copy-start.12
  551.8 27.4 %copy-start.16 = (bf16[64,2048]{1,0:T(8,128)(2,1)S(1)}, bf16[64,2048]{1,0:T(8,128)(2,1)}, u32[]{:S(2)}) copy-start(bf16[64,2048]{1,0:T(8,128)(2,1)} %copy-done.15) | copy-start | bytes 786436
  555.7 83.5 %reduce-scatter.17.cloned.1.call-start = ((), (), s32[]{:S(2)}) async-start(), calls=%async_computation.15 | async-start | bytes 786432 | tf_op jit(solution)/shard_map/reduce_scatter | solution.py:55
  580.3 7.9 %collective-permute-start.4 = (bf16[64,2048]{1,0:T(8,128)(2,1)S(1)}, bf16[64,2048]{1,0:T(8,128)(2,1)S(1)}, u32[]{:S(2)}, u32[]{:S(2)}) collective-permute-start(bf16[64,2048]{1,0:T(8,128)(2,1)S(1)} %get-tuple-element.6), channel_id=1, source_target_pairs={{0,64},{64,128},{128,192},{1,65},{65,129},{129,193},{2,66},{66,130... | collective-permute-start | bytes 786440 | tf_op jit(solution)/shard_map/ppermute | solution.py:13
  588.2 7.3 %copy-start.5 = (bf16[64,2048]{1,0:T(8,128)(2,1)}, bf16[64,2048]{1,0:T(8,128)(2,1)S(1)}, u32[]{:S(2)}) copy-start(bf16[64,2048]{1,0:T(8,128)(2,1)S(1)} %collective-permute-done.4) | copy-start | bytes 786436
  602.4 4.7 copy-start.8
  611.7 27.4 %copy-start.6 = (bf16[64,2048]{1,0:T(8,128)(2,1)S(1)}, bf16[64,2048]{1,0:T(8,128)(2,1)}, u32[]{:S(2)}) copy-start(bf16[64,2048]{1,0:T(8,128)(2,1)} %copy-done.5) | copy-start | bytes 786436
Sparse Core Ops, SparseCore 0:
  9.9 133.3 all-gather.3
  145.8 85.0 all-gather.5
  233.5 83.4 all-gather.7
  320.9 15.8 reduce-scatter.6
  374.1 23.3 reduce-scatter.8
  435.7 23.3 reduce-scatter.10
  495.6 23.3 reduce-scatter.12
  555.8 23.3 reduce-scatter.14
  615.7 23.3 reduce-scatter.16
